TPU v7x, 256 devices: a whole 4x4x8 slice. The times are simulated.
256 devices in a mesh: dp: 16 (over z, core), expert: 16 (over y, x).
Axes of the slice: x: 4, y: 4, z: 8, core: 2. Of those that a mesh axis runs over, the one named last changes fastest.
Arguments:
- ssm_state: bfloat16 [1024, 16, 4096], P('expert', None, 'dp'), may hold values from -6 to 6
- conv_state: bfloat16 [1024, 3, 4096], P('expert', None, 'dp'), may hold values from -6 to 6
- new_slot: int32 [1024], replicated, may hold values from 0 to 1023, as said below
- conv_input: bfloat16 [1024, 4096], P('expert', 'dp'), may hold values from -6 to 6
- gate_input: bfloat16 [1024, 4096], P('expert', 'dp'), may hold values from -6 to 6
- conv_weight: float32 [4, 4096], P(None, 'dp'), may hold values from -3 to 3
- conv_bias: float32 [4096], P('dp'), may hold values from -3 to 3
- x_proj_weight: bfloat16 [4096, 288], P('dp'), may hold values from -0.09375 to 0.09375
- step_weight: bfloat16 [256, 4096], P(None, 'dp'), may hold values from -0.375 to 0.375
- step_bias: float32 [4096], P('dp'), may hold values from -3 to -0.5
- decay_log: float32 [16, 4096], P(None, 'dp'), may hold values from 0 to 2
- skip_gain: float32 [4096], P('dp'), may hold values from 0.5 to 1.5
- out_proj_weight: bfloat16 [4096, 4096], P('dp', 'expert'), may hold values from -0.09375 to 0.09375
- residual: bfloat16 [1024, 4096], P(None, 'expert'), may hold values from -6 to 6
- norm_gain: float32 [4096], replicated, may hold values from 0.1 to 1.9
- routes: int32 [1024, 2], replicated, may hold values from 0 to 15, all different within a row; in each aligned block of 64 rows (0 to 63, 64 to 127, ...) at most 20 rows name the same one
- gate_weight: float32 [1024, 2], replicated, may hold values from 0.1 to 0.9
- expert_gate: bfloat16 [16, 4096, 7168], P('expert', None, 'dp'), may hold values from -0.09375 to 0.09375
- expert_up: bfloat16 [16, 4096, 7168], P('expert', None, 'dp'), may hold values from -0.09375 to 0.09375
- expert_down: bfloat16 [16, 7168, 4096], P('expert', 'dp'), may hold values from -0.0625 to 0.0625
Outputs:
- ssm_new: bfloat16 [1024, 16, 4096], P('expert', None, 'dp')
- conv_new: bfloat16 [1024, 3, 4096], P('expert', None, 'dp')
- layer_out: bfloat16 [1024, 4096], P(None, 'expert')
Inputs may be any that keep to these rules, and one draw needn't show every extreme that they name: new_slot is a permutation of the 1024 slots; slot s belongs to expert index s // 64. Of the 64 old slots of one expert index, at most 8 get new slots of any one expert index, and exactly 8 those of some expert index; every expert index sends the same multiset of such counts. `routes`: each row names 2 different experts; within each aligned block of 64 rows (the rows of one expert index) no expert is named by more than 20 rows, a bound that some block reaches.
All inputs are finite; a program needn't handle non-finite values.
Results may differ from a plain program's by a relative error of at most 0.012.
Values may be sent and summed in bfloat16 or wider, within the bound.
A program may use at most 128 MiB of HBM per device.

v0:
```python
import jax
import jax.numpy as jnp
from jax import lax
from jax.sharding import PartitionSpec as P


def dp_total(values):
    return lax.psum(values, "dp")


def body(
    ssm_state,
    conv_state,
    new_slot,
    conv_input,
    gate_input,
    conv_weight,
    conv_bias,
    x_proj_weight,
    step_weight,
    step_bias,
    decay_log,
    skip_gain,
    out_proj_weight,
    residual,
    norm_gain,
    routes,
    gate_weight,
    expert_gate,
    expert_up,
    expert_down,
):
    row_count, state_dim, channels = ssm_state.shape
    owners = lax.axis_size("expert")
    own_index = lax.axis_index("expert")
    move_cap = 2 * row_count // owners
    slot_count = owners * move_cap
    my_slots = lax.dynamic_slice_in_dim(new_slot, own_index * row_count, row_count)
    target = my_slots // row_count
    target_hot = (target[:, None] == jnp.arange(owners)[None, :]).astype(jnp.int32)
    earlier = jnp.sum((jnp.cumsum(target_hot, axis=0) - target_hot) * target_hot, axis=1)
    send_slot = target * move_cap + earlier
    send_hot = (jnp.arange(slot_count)[:, None] == send_slot[None, :]).astype(jnp.bfloat16)
    packed_ssm = (
        jnp.dot(send_hot, ssm_state.reshape(row_count, -1), preferred_element_type=jnp.float32)
        .astype(jnp.bfloat16)
        .reshape(owners, move_cap, -1)
    )
    packed_conv = (
        jnp.dot(send_hot, conv_state.reshape(row_count, -1), preferred_element_type=jnp.float32)
        .astype(jnp.bfloat16)
        .reshape(owners, move_cap, -1)
    )
    recv_ssm, recv_conv = (
        lax.all_to_all(packed_ssm, "expert", split_axis=0, concat_axis=0, tiled=True),
        lax.all_to_all(packed_conv, "expert", split_axis=0, concat_axis=0, tiled=True),
    )
    arriving = (new_slot // row_count == own_index).astype(jnp.int32).reshape(owners, row_count)
    arrive_rank = (jnp.cumsum(arriving, axis=1) - arriving).reshape(-1)
    source_ids = jnp.arange(owners * row_count) // row_count
    recv_slot = source_ids * move_cap + arrive_rank
    new_place = new_slot % row_count
    place_rows = (
        (new_place[None, :] == jnp.arange(row_count)[:, None])
        & (arriving.reshape(-1)[None, :] == 1)
    ).astype(jnp.bfloat16)
    place_slots = (recv_slot[:, None] == jnp.arange(slot_count)[None, :]).astype(jnp.bfloat16)
    place_hot = jnp.dot(place_rows, place_slots, preferred_element_type=jnp.float32).astype(
        jnp.bfloat16
    )
    moved_ssm = (
        jnp.dot(place_hot, recv_ssm.reshape(slot_count, -1), preferred_element_type=jnp.float32)
        .astype(jnp.bfloat16)
        .reshape(row_count, state_dim, channels)
    )
    moved_conv = (
        jnp.dot(place_hot, recv_conv.reshape(slot_count, -1), preferred_element_type=jnp.float32)
        .astype(jnp.bfloat16)
        .reshape(row_count, -1, channels)
    )
    window = jnp.concatenate([moved_conv, conv_input[:, None, :]], axis=1)
    conv_new = window[:, 1:, :]
    conv_sum = (
        jnp.sum(window.astype(jnp.float32) * conv_weight[None, :, :], axis=1) + conv_bias[None, :]
    )
    activated = jax.nn.silu(conv_sum).astype(jnp.bfloat16)
    projected = dp_total(jnp.dot(activated, x_proj_weight, preferred_element_type=jnp.float32))
    rank_dim = step_weight.shape[0]
    step_low = projected[:, :rank_dim]
    b_coef = projected[:, rank_dim : rank_dim + state_dim]
    c_coef = projected[:, rank_dim + state_dim :]
    step_norm = (
        step_low * lax.rsqrt(jnp.mean(step_low * step_low, axis=1, keepdims=True) + 1e-06)
    ).astype(jnp.bfloat16)
    step_size = jax.nn.softplus(
        jnp.dot(step_norm, step_weight, preferred_element_type=jnp.float32) + step_bias[None, :]
    )
    act_float = activated.astype(jnp.float32)
    decays = jnp.exp(step_size[:, None, :] * (-jnp.exp(decay_log))[None, :, :])
    states = (
        decays * moved_ssm.astype(jnp.float32)
        + (step_size * act_float)[:, None, :] * b_coef[:, :, None]
    )
    ssm_new = states.astype(jnp.bfloat16)
    gated_out = (
        (jnp.sum(c_coef[:, :, None] * states, axis=1) + skip_gain[None, :] * act_float)
        * jax.nn.silu(gate_input.astype(jnp.float32))
    ).astype(jnp.bfloat16)
    mamba_mix = dp_total(
        jnp.dot(
            lax.all_gather(gated_out, "expert", axis=0, tiled=True),
            out_proj_weight,
            preferred_element_type=jnp.float32,
        )
    )
    stream = (residual.astype(jnp.float32) + mamba_mix).astype(jnp.bfloat16)
    top_count = routes.shape[1]
    width = stream.shape[1]
    capacity = min(row_count, 5 * row_count * top_count // (2 * owners))
    expert_hot = (
        (routes[:, :, None] == jnp.arange(owners)[None, None, :])
        .astype(jnp.int32)
        .reshape(owners, row_count * top_count, owners)
    )
    prior = jnp.sum((jnp.cumsum(expert_hot, axis=1) - expert_hot) * expert_hot, axis=2)
    slot_of = (routes.reshape(owners, row_count * top_count) * capacity + prior).reshape(
        owners, row_count, top_count
    )
    matches = slot_of[:, :, :, None] == jnp.arange(owners * capacity)[None, None, None, :]
    dispatch_hot = (
        jnp.any(matches, axis=2).astype(jnp.bfloat16).reshape(owners, row_count, owners, capacity)
    )
    combine_w = jnp.sum(
        jnp.where(matches, gate_weight.reshape(owners, row_count, top_count)[:, :, :, None], 0.0),
        axis=2,
    ).reshape(owners, row_count, owners, capacity)
    outgoing = jnp.einsum(
        "orec,ord->eocd",
        dispatch_hot,
        stream.reshape(owners, row_count, width),
        preferred_element_type=jnp.float32,
    ).astype(jnp.bfloat16)
    arrived = lax.all_to_all(outgoing, "expert", split_axis=0, concat_axis=3, tiled=True)
    tokens = arrived.reshape(owners * capacity, -1).astype(jnp.float32)
    normed = (
        tokens
        * lax.rsqrt(jnp.mean(tokens * tokens, axis=1, keepdims=True) + 1e-05)
        * norm_gain[None, :]
    ).astype(jnp.bfloat16)
    gate_val = jnp.dot(normed, expert_gate[0], preferred_element_type=jnp.float32)
    up_val = jnp.dot(normed, expert_up[0], preferred_element_type=jnp.float32)
    hidden = (jax.nn.silu(gate_val) * up_val).astype(jnp.bfloat16)
    partial_out = jnp.dot(hidden, expert_down[0], preferred_element_type=jnp.float32).reshape(
        owners, capacity, -1
    )
    summed = dp_total(partial_out)
    returned = lax.all_to_all(
        summed.astype(jnp.bfloat16), "expert", split_axis=2, concat_axis=0, tiled=True
    ).astype(summed.dtype)
    expert_mix = jnp.einsum(
        "orec,eocd->ord",
        combine_w,
        returned.reshape(owners, owners, capacity, width),
        precision=lax.Precision.HIGHEST,
        preferred_element_type=jnp.float32,
    )
    layer_out = (stream.astype(jnp.float32) + expert_mix.reshape(-1, width)).astype(jnp.bfloat16)
    return (ssm_new, conv_new, layer_out)


def solution(mesh):
    in_specs = (
        P("expert", None, "dp"),
        P("expert", None, "dp"),
        P(),
        P("expert", "dp"),
        P("expert", "dp"),
        P(None, "dp"),
        P("dp"),
        P("dp", None),
        P(None, "dp"),
        P("dp"),
        P(None, "dp"),
        P("dp"),
        P("dp", "expert"),
        P(None, "expert"),
        P(),
        P(),
        P(),
        P("expert", None, "dp"),
        P("expert", None, "dp"),
        P("expert", "dp", None),
    )
    out_specs = (P("expert", None, "dp"), P("expert", None, "dp"), P(None, "expert"))
    return jax.shard_map(body, mesh=mesh, in_specs=in_specs, out_specs=out_specs, check_vma=False)
```

profile of v0, /device:TPU:97, one launch (start us, length us, event | category | flops | bytes accessed | tf_op | source)
XLA Modules:
  0.0 587.0 jit_solution(9232045870672755872)
XLA Ops:
  10.9 6.9 %all-to-all-start = ((bf16[16,8,768]{2,1,0:T(8,128)(2,1)}), bf16[16,8,768]{2,1,0:T(8,128)(2,1)S(1)}, u32[]{:S(2)}, u32[]{:S(2)}) async-start(bf16[16,8,768]{2,1,0:T(8,128)(2,1)} %fusion.30), calls=%async_computation | async-start | bytes 393216 | tf_op jit(solution)/shard_map/all_to_all | solution.py:56
  19.6 1.3 copy.108
  20.9 1.4 fusion.3
  22.7 2.3 all-to-all-done
  25.0 4.4 all-to-all-start.1
  30.9 108.3 %all-reduce.4.cloned.1.call-done = f32[64,288]{1,0:T(8,128)} async-done(((f32[64,288]{1,0:T(8,128)}), f32[64,288]{1,0:T(8,128)}) %all-reduce.4.cloned.1.call-update) | async-done | bytes 73744 | tf_op jit(solution)/shard_map/psum | solution.py:8
  141.1 1.1 convert_multiply_fusion.4
  142.9 1.3 multiply_reduce_fusion
  144.2 19.4 %all_gather.3 = bf16[1024,256]{1,0:T(8,128)(2,1)S(1)} all-gather(bf16[64,256]{1,0:T(8,128)(2,1)S(1)} %fusion.46), channel_id=1, replica_groups=mesh['dp'=16,'expert'=16] {'expert'}, dimensions={0}, use_global_device_ids=true | all-gather | bytes 557056 | tf_op jit(solution)/shard_map/all_gather | solution.py:111
  163.6 1.3 fusion.66
  165.7 2.8 select_reduce_fusion.1
  169.2 1.3 copy.91
  170.6 109.3 %all-reduce.6.cloned.1.call-done = f32[1024,256]{1,0:T(8,128)} async-done(((f32[1024,256]{1,0:T(8,128)}), f32[1024,256]{1,0:T(8,128)}) %all-reduce.6.cloned.1.call-update) | async-done | bytes 1048592 | tf_op jit(solution)/shard_map/psum | solution.py:8
  279.8 1.3 add_convert_fusion
  282.1 3.0 copy.93
  285.1 6.7 %all-to-all-start.2 = ((bf16[16,16,20,256]{3,1,2,0:T(8,128)(2,1)}), bf16[16,16,20,256]{3,1,2,0:T(8,128)(2,1)S(1)}, u32[]{:S(2)}, u32[]{:S(2)}) async-start(bf16[16,16,20,256]{3,1,2,0:T(8,128)(2,1)} %copy.93), calls=%async_computation.2 | async-start | bytes 5242880 | tf_op jit(solution)/shard_map/all_to_all | solution.py:143
  291.8 41.7 %all-to-all-done.2 = bf16[16,16,20,256]{3,1,2,0:T(8,128)(2,1)S(1)} async-done(((bf16[16,16,20,256]{3,1,2,0:T(8,128)(2,1)}), bf16[16,16,20,256]{3,1,2,0:T(8,128)(2,1)S(1)}, u32[]{:S(2)}, u32[]{:S(2)}) %all-to-all-start.2) | async-done | bytes 2621472 | tf_op jit(solution)/shard_map/all_to_all | solution.py:143
  334.9 1.5 copy.94
  336.4 1.2 copy.110
  338.4 1.5 fusion.9
  340.5 1.5 fusion.27
  342.1 5.9 %fusion.5 = f32[16,20,4096]{2,0,1:T(8,128)} fusion(bf16[1,448,4096]{2,1,0:T(8,128)(2,1)} %param.39, bf16[16,20,448]{2,1,0:T(8,128)(2,1)S(1)} %dot_general.52), kind=kOutput, calls=%fused_computation.9 | convolution fusion | flops 1174405120 | bytes 9199616 | tf_op jit(solution)/shard_map/dot_general | solution.py:153
  348.0 74.7 %all-reduce.7 = bf16[16,20,4096]{2,0,1:T(8,128)(2,1)S(1)} all-reduce(f32[16,20,4096]{2,0,1:T(8,128)} %fusion.5), channel_id=1, replica_groups=mesh['dp'=16,'expert'=16] {'dp'}, use_global_device_ids=true, to_apply=%region_13.14 | all-reduce | flops 1310720 | bytes 7864320 | tf_op jit(solution)/shard_map/psum | solution.py:8
  422.7 14.9 %copy.96 = bf16[16,20,4096]{1,0,2:T(8,128)(2,1)} copy(bf16[16,20,4096]{2,0,1:T(8,128)(2,1)S(1)} %all-reduce.7) | data formatting | bytes 5242880 | tf_op jit(solution)/shard_map/convert_element_type | solution.py:158
  437.6 34.7 %reshape.150 = bf16[16,2,40960]{2,1,0:T(2,128)(2,1)} reshape(bf16[4096,16,20]{2,1,0:T(8,128)(2,1)} %bitcast.85) | data formatting | bytes 5242880
  472.3 4.1 all-to-all-start.3
  476.5 2.0 select_reduce_fusion
  478.5 3.1 copy.90
  482.4 35.1 %all-to-all-done.3 = bf16[16,2,40960]{2,1,0:T(2,128)(2,1)S(1)} async-done(((bf16[16,2,40960]{2,1,0:T(2,128)(2,1)}), bf16[16,2,40960]{2,1,0:T(2,128)(2,1)S(1)}, u32[]{:S(2)}, u32[]{:S(2)}) %all-to-all-start.3) | async-done | bytes 2621472 | tf_op jit(solution)/shard_map/all_to_all | solution.py:157
  517.5 42.4 %reshape.151 = bf16[4096,16,20]{2,1,0:T(8,128)(2,1)} reshape(bf16[16,2,40960]{2,1,0:T(2,128)(2,1)S(1)} %all-to-all-done.3) | data formatting | bytes 5242880
  559.9 14.0 %copy.98 = bf16[16,20,16,256]{3,2,1,0:T(8,128)(2,1)S(1)} copy(bf16[16,20,16,256]{1,0,3,2:T(8,128)(2,1)} %bitcast.86) | data formatting | bytes 5242880 | tf_op jit(solution)/shard_map/all_to_all | solution.py:157
  573.9 5.3 fusion.15
  (84 shorter events, 16.9 us)
Async XLA Ops:
  7.2 22.8 %copy-start = (bf16[256,288]{0,1:T(8,128)(2,1)S(1)}, bf16[256,288]{0,1:T(8,128)(2,1)}, u32[]{:S(2)}) copy-start(bf16[256,288]{0,1:T(8,128)(2,1)} %param.27) | copy-start | bytes 442372
  7.2 15.1 %copy-start.5 = (bf16[64,256]{1,0:T(8,128)(2,1)S(1)}, bf16[64,256]{1,0:T(8,128)(2,1)}, u32[]{:S(2)}) copy-start(bf16[64,256]{1,0:T(8,128)(2,1)} %param.23) | copy-start | bytes 98308
  10.9 18.7 %copy-start.10 = (f32[4,256]{1,0:T(4,128)S(1)}, f32[4,256]{1,0:T(4,128)}, u32[]{:S(2)}) copy-start(f32[4,256]{1,0:T(4,128)} %param.25) | copy-start | bytes 12292
  10.9 19.0 %copy-start.11 = (f32[256]{0:T(256)S(1)}, f32[256]{0:T(256)}, u32[]{:S(2)}) copy-start(f32[256]{0:T(256)} %param.26) | copy-start | bytes 3076
  10.9 14.1 %all-to-all-start = ((bf16[16,8,768]{2,1,0:T(8,128)(2,1)}), bf16[16,8,768]{2,1,0:T(8,128)(2,1)S(1)}, u32[]{:S(2)}, u32[]{:S(2)}) async-start(bf16[16,8,768]{2,1,0:T(8,128)(2,1)} %fusion.30), calls=%async_computation | async-start | bytes 393216 | tf_op jit(solution)/shard_map/all_to_all | solution.py:56
  19.6 11.3 %copy-start.7 = (f32[16,256]{1,0:T(8,128)S(1)}, f32[16,256]{1,0:T(8,128)}, u32[]{:S(2)}) copy-start(f32[16,256]{1,0:T(8,128)} %param.30) | copy-start | bytes 49156
  19.6 121.5 %copy-start.15 = (bf16[256,256]{1,0:T(8,128)(2,1)S(1)}, bf16[256,256]{1,0:T(8,128)(2,1)}, u32[]{:S(2)}) copy-start(bf16[256,256]{1,0:T(8,128)(2,1)} %param.28) | copy-start | bytes 393220
  19.6 121.5 %copy-start.16 = (f32[256]{0:T(256)S(1)}, f32[256]{0:T(256)}, u32[]{:S(2)}) copy-start(f32[256]{0:T(256)} %param.29) | copy-start | bytes 3076
  25.0 117.2 %all-to-all-start.1 = ((bf16[16,8,4096]{2,1,0:T(8,128)(2,1)}), bf16[16,8,4096]{2,1,0:T(8,128)(2,1)S(1)}, u32[]{:S(2)}, u32[]{:S(2)}) async-start(bf16[16,8,4096]{2,1,0:T(8,128)(2,1)} %fusion.3), calls=%async_computation.1 | async-start | bytes 2097152 | tf_op jit(solution)/shard_map/all_to_all | solution.py:55
  29.4 109.9 %all-reduce.4.cloned.1.call-start = ((), (), s32[]{:S(2)}) async-start(), calls=%async_computation.4 | async-start | bytes 196608 | tf_op jit(solution)/shard_map/psum | solution.py:8
  30.8 249.0 %all-reduce.6.cloned.1.call-start = ((), (), s32[]{:S(2)}) async-start(), calls=%async_computation.5 | async-start | bytes 2097152 | tf_op jit(solution)/shard_map/psum | solution.py:8
  142.2 2.0 copy-start.6
  142.2 2.0 copy-start.12
  142.2 21.4 %copy-start.3 = (bf16[256,256]{1,0:T(8,128)(2,1)S(1)}, bf16[256,256]{1,0:T(8,128)(2,1)}, u32[]{:S(2)}) copy-start(bf16[256,256]{1,0:T(8,128)(2,1)} %param.32) | copy-start | bytes 393220
  142.8 22.1 %copy-start.4 = (s32[1024,2]{0,1:T(2,128)S(1)}, s32[1024,2]{0,1:T(2,128)}, u32[]{:S(2)}) copy-start(s32[1024,2]{0,1:T(2,128)} %param.35) | copy-start | bytes 24580
  144.2 135.6 %copy-start.2 = (bf16[1024,256]{1,0:T(8,128)(2,1)S(1)}, bf16[1024,256]{1,0:T(8,128)(2,1)}, u32[]{:S(2)}) copy-start(bf16[1024,256]{1,0:T(8,128)(2,1)} %param.33) | copy-start | bytes 1572868
  285.1 6.7 %copy-start.8 = (f32[4096]{0:T(1024)S(1)}, f32[4096]{0:T(1024)}, u32[]{:S(2)}) copy-start(f32[4096]{0:T(1024)} %param.34) | copy-start | bytes 49156
  285.1 48.4 %all-to-all-start.2 = ((bf16[16,16,20,256]{3,1,2,0:T(8,128)(2,1)}), bf16[16,16,20,256]{3,1,2,0:T(8,128)(2,1)S(1)}, u32[]{:S(2)}, u32[]{:S(2)}) async-start(bf16[16,16,20,256]{3,1,2,0:T(8,128)(2,1)} %copy.93), calls=%async_computation.2 | async-start | bytes 5242880 | tf_op jit(solution)/shard_map/all_to_all | solution.py:143
  336.4 2.0 copy-start.13
  338.4 2.0 copy-start.14
  472.3 4.1 copy-start.9
  472.3 45.2 %all-to-all-start.3 = ((bf16[16,2,40960]{2,1,0:T(2,128)(2,1)}), bf16[16,2,40960]{2,1,0:T(2,128)(2,1)S(1)}, u32[]{:S(2)}, u32[]{:S(2)}) async-start(bf16[16,2,40960]{2,1,0:T(2,128)(2,1)} %reshape.150), calls=%async_computation.3 | async-start | bytes 5242880 | tf_op jit(solution)/shard_map/all_to_all | solution.py:157
  573.9 6.2 %copy-start.1 = (bf16[256,288]{0,1:T(8,128)(2,1)S(1)}, bf16[256,288]{0,1:T(8,128)(2,1)}, u32[]{:S(2)}) copy-start(bf16[256,288]{0,1:T(8,128)(2,1)} %param.27) | copy-start | bytes 442372
Sparse Core Ops, SparseCore 0:
  33.1 106.0 all-reduce.3
  165.1 114.7 all-reduce.5
where the time goes:
time: 588 us; the launch traced here: 587 us
  waiting for transfers between devices  297 us (51%)
  local copies, waits for them, and re-layouts  123 us (21%)
  blocking collectives  94 us (16%)
  starting transfers between devices  22.1 us (4%)
  matrix products  21.5 us (4%)
  other arithmetic  15.4 us (3%)
  between operations  14.5 us (2%)
    psum x2, waiting for transfers between devices, dp_total(): return lax.psum(values, 'dp')  218 us
    unnamed x41, local copies, waits for them, and re-layouts  82.2 us
    psum x1, blocking collectives, dp_total(): return lax.psum(values, 'dp')  74.7 us
    all_to_all x1, waiting for transfers between devices, body(): lax.all_to_all(outgoing, 'expert', split_axis=0, concat_axis=3, tiled=True)  41.7 us
    all_to_all x1, waiting for transfers between devices, body(): lax.all_to_all(summed.astype(jnp.bfloat16), 'expert', split_axis=2, conca...  35.1 us
    all_gather x1, blocking collectives, body(): lax.all_gather(gated_out, 'expert', axis=0, tiled=True)  19.4 us
    convert_element_type x1, local copies, waits for them, and re-layouts, body(): summed.astype(jnp.bfloat16)  14.9 us
    all_to_all x1, local copies, waits for them, and re-layouts, body(): lax.all_to_all(summed.astype(jnp.bfloat16), 'expert', split_axis=2, conca...  14 us
  transfers between devices with their start and end apart: 6, of which 5 were waited for; matrix products, arithmetic and copies ran while one was open for 4% of the time, Pallas kernels for 0%

commit v1 on v0

--- a/solution.py
+++ b/solution.py
@@ -140,7 +140,12 @@
         stream.reshape(owners, row_count, width),
         preferred_element_type=jnp.float32,
     ).astype(jnp.bfloat16)
-    arrived = lax.all_to_all(outgoing, "expert", split_axis=0, concat_axis=3, tiled=True)
+    arrived = jnp.concatenate(
+        lax.all_to_all(
+            jnp.stack(jnp.split(outgoing, lax.axis_size("expert"), axis=0)), "expert", 0, 0
+        ),
+        axis=3,
+    )
     tokens = arrived.reshape(owners * capacity, -1).astype(jnp.float32)
     normed = (
         tokens

time: 588 us -> 588 us (level)
    unnamed x41 -> x56, local copies, waits for them, and re-layouts: 82.2 us -> 82.4 us
where the time goes in v1:
time: 588 us; the launch traced here: 587 us
  waiting for transfers between devices  297 us (51%)
  local copies, waits for them, and re-layouts  122 us (21%)
  blocking collectives  94 us (16%)
  starting transfers between devices  22.1 us (4%)
  matrix products  21.5 us (4%)
  other arithmetic  15.4 us (3%)
  between operations  14.6 us (2%)
    psum x2, waiting for transfers between devices, dp_total(): return lax.psum(values, 'dp')  218 us
    unnamed x56, local copies, waits for them, and re-layouts  82.4 us
    psum x1, blocking collectives, dp_total(): return lax.psum(values, 'dp')  74.7 us
    all_to_all x1, waiting for transfers between devices, body(): lax.all_to_all(jnp.stack(jnp.split(outgoing, lax.axis_size('expert'), axi...  41.7 us
    all_to_all x1, waiting for transfers between devices, body(): lax.all_to_all(summed.astype(jnp.bfloat16), 'expert', split_axis=2, conca...  35.1 us
    all_gather x1, blocking collectives, body(): lax.all_gather(gated_out, 'expert', axis=0, tiled=True)  19.4 us
    convert_element_type x1, local copies, waits for them, and re-layouts, body(): summed.astype(jnp.bfloat16)  14.9 us
    all_to_all x1, local copies, waits for them, and re-layouts, body(): lax.all_to_all(summed.astype(jnp.bfloat16), 'expert', split_axis=2, conca...  14 us
  transfers between devices with their start and end apart: 6, of which 5 were waited for; matrix products, arithmetic and copies ran while one was open for 4% of the time, Pallas kernels for 0%

profile of v1, /device:TPU:97, one launch (start us, length us, event | category | flops | bytes accessed | tf_op | source)
XLA Modules:
  0.0 586.7 jit_solution(7184945800215089622)
XLA Ops:
  10.9 6.9 %all-to-all-start = ((bf16[16,8,768]{2,1,0:T(8,128)(2,1)}), bf16[16,8,768]{2,1,0:T(8,128)(2,1)S(1)}, u32[]{:S(2)}, u32[]{:S(2)}) async-start(bf16[16,8,768]{2,1,0:T(8,128)(2,1)} %fusion.30), calls=%async_computation | async-start | bytes 393216 | tf_op jit(solution)/shard_map/all_to_all | solution.py:56
  19.6 1.3 copy.213
  20.9 1.4 fusion.3
  22.7 2.3 all-to-all-done
  25.0 4.4 all-to-all-start.1
  30.9 108.3 %all-reduce.4.cloned.1.call-done = f32[64,288]{1,0:T(8,128)} async-done(((f32[64,288]{1,0:T(8,128)}), f32[64,288]{1,0:T(8,128)}) %all-reduce.4.cloned.1.call-update) | async-done | bytes 73744 | tf_op jit(solution)/shard_map/psum | solution.py:8
  141.1 1.1 convert_multiply_fusion.4
  142.9 1.3 multiply_reduce_fusion
  144.2 19.4 %all_gather.3 = bf16[1024,256]{1,0:T(8,128)(2,1)S(1)} all-gather(bf16[64,256]{1,0:T(8,128)(2,1)S(1)} %fusion.62), channel_id=1, replica_groups=mesh['dp'=16,'expert'=16] {'expert'}, dimensions={0}, use_global_device_ids=true | all-gather | bytes 557056 | tf_op jit(solution)/shard_map/all_gather | solution.py:111
  163.6 1.3 fusion.82
  165.7 2.8 select_reduce_fusion.1
  169.2 1.3 copy.166
  170.6 109.3 %all-reduce.6.cloned.1.call-done = f32[1024,256]{1,0:T(8,128)} async-done(((f32[1024,256]{1,0:T(8,128)}), f32[1024,256]{1,0:T(8,128)}) %all-reduce.6.cloned.1.call-update) | async-done | bytes 1048592 | tf_op jit(solution)/shard_map/psum | solution.py:8
  279.8 1.3 add_convert_fusion
  282.6 2.2 copy.183
  284.8 6.7 %all-to-all-start.2 = ((bf16[16,1,16,20,256]{4,2,3,1,0:T(8,128)(2,1)}), bf16[16,1,16,20,256]{4,2,3,1,0:T(8,128)(2,1)S(1)}, u32[]{:S(2)}, u32[]{:S(2)}) async-start(bf16[16,1,16,20,256]{4,2,3,1,0:T(8,128)(2,1)} %copy.183), calls=%async_computation.2 | async-start | bytes 5242880 | tf_op jit(solution)/shard_map/all_to_all | solution.py:144
  291.5 41.7 %all-to-all-done.2 = bf16[16,1,16,20,256]{4,2,3,1,0:T(8,128)(2,1)S(1)} async-done(((bf16[16,1,16,20,256]{4,2,3,1,0:T(8,128)(2,1)}), bf16[16,1,16,20,256]{4,2,3,1,0:T(8,128)(2,1)S(1)}, u32[]{:S(2)}, u32[]{:S(2)}) %all-to-all-start.2) | async-done | bytes 2621472 | tf_op jit(solution)/shard_map/all_to_all | solution.py:144
  334.6 1.5 copy.184
  336.1 1.2 copy.215
  338.1 1.5 fusion.9
  340.1 1.5 fusion.27
  341.8 5.9 %fusion.5 = f32[16,20,4096]{2,0,1:T(8,128)} fusion(bf16[1,448,4096]{2,1,0:T(8,128)(2,1)} %param.39, bf16[16,20,448]{2,1,0:T(8,128)(2,1)S(1)} %dot_general.52), kind=kOutput, calls=%fused_computation.9 | convolution fusion | flops 1174405120 | bytes 9199616 | tf_op jit(solution)/shard_map/dot_general | solution.py:158
  347.7 74.7 %all-reduce.7 = bf16[16,20,4096]{2,0,1:T(8,128)(2,1)S(1)} all-reduce(f32[16,20,4096]{2,0,1:T(8,128)} %fusion.5), channel_id=1, replica_groups=mesh['dp'=16,'expert'=16] {'dp'}, use_global_device_ids=true, to_apply=%region_13.14 | all-reduce | flops 1310720 | bytes 7864320 | tf_op jit(solution)/shard_map/psum | solution.py:8
  422.4 14.9 %copy.186 = bf16[16,20,4096]{1,0,2:T(8,128)(2,1)} copy(bf16[16,20,4096]{2,0,1:T(8,128)(2,1)S(1)} %all-reduce.7) | data formatting | bytes 5242880 | tf_op jit(solution)/shard_map/convert_element_type | solution.py:163
  437.2 34.7 %reshape.146 = bf16[16,2,40960]{2,1,0:T(2,128)(2,1)} reshape(bf16[4096,16,20]{2,1,0:T(8,128)(2,1)} %bitcast.175) | data formatting | bytes 5242880
  471.9 4.1 all-to-all-start.3
  476.2 2.0 select_reduce_fusion
  478.1 3.1 copy.165
  482.1 35.1 %all-to-all-done.3 = bf16[16,2,40960]{2,1,0:T(2,128)(2,1)S(1)} async-done(((bf16[16,2,40960]{2,1,0:T(2,128)(2,1)}), bf16[16,2,40960]{2,1,0:T(2,128)(2,1)S(1)}, u32[]{:S(2)}, u32[]{:S(2)}) %all-to-all-start.3) | async-done | bytes 2621472 | tf_op jit(solution)/shard_map/all_to_all | solution.py:162
  517.2 42.4 %reshape.147 = bf16[4096,16,20]{2,1,0:T(8,128)(2,1)} reshape(bf16[16,2,40960]{2,1,0:T(2,128)(2,1)S(1)} %all-to-all-done.3) | data formatting | bytes 5242880
  559.6 14.0 %copy.188 = bf16[16,20,16,256]{3,2,1,0:T(8,128)(2,1)S(1)} copy(bf16[16,20,16,256]{1,0,3,2:T(8,128)(2,1)} %bitcast.176) | data formatting | bytes 5242880 | tf_op jit(solution)/shard_map/all_to_all | solution.py:162
  573.6 5.3 fusion.15
  (100 shorter events, 17.2 us)
Async XLA Ops:
  7.2 22.8 %copy-start = (bf16[256,288]{0,1:T(8,128)(2,1)S(1)}, bf16[256,288]{0,1:T(8,128)(2,1)}, u32[]{:S(2)}) copy-start(bf16[256,288]{0,1:T(8,128)(2,1)} %param.27) | copy-start | bytes 442372
  7.2 15.1 %copy-start.5 = (bf16[64,256]{1,0:T(8,128)(2,1)S(1)}, bf16[64,256]{1,0:T(8,128)(2,1)}, u32[]{:S(2)}) copy-start(bf16[64,256]{1,0:T(8,128)(2,1)} %param.23) | copy-start | bytes 98308
  10.9 18.7 %copy-start.10 = (f32[4,256]{1,0:T(4,128)S(1)}, f32[4,256]{1,0:T(4,128)}, u32[]{:S(2)}) copy-start(f32[4,256]{1,0:T(4,128)} %param.25) | copy-start | bytes 12292
  10.9 19.0 %copy-start.11 = (f32[256]{0:T(256)S(1)}, f32[256]{0:T(256)}, u32[]{:S(2)}) copy-start(f32[256]{0:T(256)} %param.26) | copy-start | bytes 3076
  10.9 14.1 %all-to-all-start = ((bf16[16,8,768]{2,1,0:T(8,128)(2,1)}), bf16[16,8,768]{2,1,0:T(8,128)(2,1)S(1)}, u32[]{:S(2)}, u32[]{:S(2)}) async-start(bf16[16,8,768]{2,1,0:T(8,128)(2,1)} %fusion.30), calls=%async_computation | async-start | bytes 393216 | tf_op jit(solution)/shard_map/all_to_all | solution.py:56
  19.6 11.3 %copy-start.7 = (f32[16,256]{1,0:T(8,128)S(1)}, f32[16,256]{1,0:T(8,128)}, u32[]{:S(2)}) copy-start(f32[16,256]{1,0:T(8,128)} %param.30) | copy-start | bytes 49156
  19.6 121.5 %copy-start.15 = (bf16[256,256]{1,0:T(8,128)(2,1)S(1)}, bf16[256,256]{1,0:T(8,128)(2,1)}, u32[]{:S(2)}) copy-start(bf16[256,256]{1,0:T(8,128)(2,1)} %param.28) | copy-start | bytes 393220
  19.6 121.5 %copy-start.16 = (f32[256]{0:T(256)S(1)}, f32[256]{0:T(256)}, u32[]{:S(2)}) copy-start(f32[256]{0:T(256)} %param.29) | copy-start | bytes 3076
  25.0 117.2 %all-to-all-start.1 = ((bf16[16,8,4096]{2,1,0:T(8,128)(2,1)}), bf16[16,8,4096]{2,1,0:T(8,128)(2,1)S(1)}, u32[]{:S(2)}, u32[]{:S(2)}) async-start(bf16[16,8,4096]{2,1,0:T(8,128)(2,1)} %fusion.3), calls=%async_computation.1 | async-start | bytes 2097152 | tf_op jit(solution)/shard_map/all_to_all | solution.py:55
  29.4 109.9 %all-reduce.4.cloned.1.call-start = ((), (), s32[]{:S(2)}) async-start(), calls=%async_computation.4 | async-start | bytes 196608 | tf_op jit(solution)/shard_map/psum | solution.py:8
  30.8 249.0 %all-reduce.6.cloned.1.call-start = ((), (), s32[]{:S(2)}) async-start(), calls=%async_computation.5 | async-start | bytes 2097152 | tf_op jit(solution)/shard_map/psum | solution.py:8
  142.2 2.0 copy-start.6
  142.2 2.0 copy-start.12
  142.2 21.4 %copy-start.3 = (bf16[256,256]{1,0:T(8,128)(2,1)S(1)}, bf16[256,256]{1,0:T(8,128)(2,1)}, u32[]{:S(2)}) copy-start(bf16[256,256]{1,0:T(8,128)(2,1)} %param.32) | copy-start | bytes 393220
  142.8 22.1 %copy-start.4 = (s32[1024,2]{0,1:T(2,128)S(1)}, s32[1024,2]{0,1:T(2,128)}, u32[]{:S(2)}) copy-start(s32[1024,2]{0,1:T(2,128)} %param.35) | copy-start | bytes 24580
  144.2 135.6 %copy-start.2 = (bf16[1024,256]{1,0:T(8,128)(2,1)S(1)}, bf16[1024,256]{1,0:T(8,128)(2,1)}, u32[]{:S(2)}) copy-start(bf16[1024,256]{1,0:T(8,128)(2,1)} %param.33) | copy-start | bytes 1572868
  284.8 6.7 %copy-start.8 = (f32[4096]{0:T(1024)S(1)}, f32[4096]{0:T(1024)}, u32[]{:S(2)}) copy-start(f32[4096]{0:T(1024)} %param.34) | copy-start | bytes 49156
  284.8 48.4 %all-to-all-start.2 = ((bf16[16,1,16,20,256]{4,2,3,1,0:T(8,128)(2,1)}), bf16[16,1,16,20,256]{4,2,3,1,0:T(8,128)(2,1)S(1)}, u32[]{:S(2)}, u32[]{:S(2)}) async-start(bf16[16,1,16,20,256]{4,2,3,1,0:T(8,128)(2,1)} %copy.183), calls=%async_computation.2 | async-start | bytes 5242880 | tf_op jit(solution)/shard_map/all_to_all | solution.py:144
  336.1 2.0 copy-start.13
  338.1 2.0 copy-start.14
  471.9 4.1 copy-start.9
  471.9 45.2 %all-to-all-start.3 = ((bf16[16,2,40960]{2,1,0:T(2,128)(2,1)}), bf16[16,2,40960]{2,1,0:T(2,128)(2,1)S(1)}, u32[]{:S(2)}, u32[]{:S(2)}) async-start(bf16[16,2,40960]{2,1,0:T(2,128)(2,1)} %reshape.146), calls=%async_computation.3 | async-start | bytes 5242880 | tf_op jit(solution)/shard_map/all_to_all | solution.py:162
  573.6 6.2 %copy-start.1 = (bf16[256,288]{0,1:T(8,128)(2,1)S(1)}, bf16[256,288]{0,1:T(8,128)(2,1)}, u32[]{:S(2)}) copy-start(bf16[256,288]{0,1:T(8,128)(2,1)} %param.27) | copy-start | bytes 442372
Sparse Core Ops, SparseCore 0:
  33.1 106.0 all-reduce.3
  165.1 114.7 all-reduce.5
